TPU v7x, 256 devices: a whole 4x4x8 slice. The times are simulated.
256 devices in a mesh: replica: 16 (over z, core), mp: 16 (over y, x).
Axes of the slice: x: 4, y: 4, z: 8, core: 2. Of those that a mesh axis runs over, the one named last changes fastest.
Arguments:
- gradients: bfloat16 [16, 8, 768, 3072], P('replica', None, 'mp'), may hold values from -6 to 6
- feedback: bfloat16 [16, 8, 768, 3072], P('replica', None, 'mp'), may hold values from -4 to 4
- right_init: bfloat16 [8, 3072, 32], replicated, may hold values from -0.109375 to 0.109375
- gram_root: float32 [8, 32, 32], replicated, as said below
- owners: int32 [8], replicated, may hold values from 0 to 15, as said below
- momentum: float32 [16, 1, 768, 3072], P('mp', None, 'replica'), may hold values from -4 to 4
- master_weights: float32 [16, 1, 768, 3072], P('mp', None, 'replica'), may hold values from -1.5 to 1.5
- vector_grads: float32 [16, 10752], P('replica', 'mp'), may hold values from -6 to 6
- vector_momentum: float32 [10752], P('mp'), may hold values from -6 to 6
- vector_params: float32 [10752], P('mp'), may hold values from -6 to 6
Outputs:
- new_feedback: bfloat16 [16, 8, 768, 3072], P('replica', None, 'mp')
- new_momentum: float32 [16, 1, 768, 3072], P('mp', None, 'replica')
- new_master: float32 [16, 1, 768, 3072], P('mp', None, 'replica')
- new_weights: bfloat16 [8, 768, 3072], P(None, 'replica')
- new_vector_momentum: float32 [10752], P('mp')
- new_vector_params: float32 [10752], P('mp')
Inputs may be any that keep to these rules, and one draw needn't show every extreme that they name: `owners`: every matrix has one owner; no owner holds more than 1 of the 8 matrices, and one owner holds exactly 1. `gram_root`: each matrix is the identity plus off-diagonal terms, times a positive scale.
All inputs are finite; a program needn't handle non-finite values.
Results may differ from a plain program's by a relative error of at most 0.007.
Values may be sent and summed in bfloat16 or wider, within the bound.
A program may use at most 192 MiB of HBM per device.

v0:
```python
import jax
import jax.numpy as jnp
from jax import lax
from jax.sharding import PartitionSpec as P


def per_device(
    gradients,
    feedback,
    right_init,
    gram_root,
    owners,
    momentum,
    master_weights,
    vector_grads,
    vector_momentum,
    vector_params,
):
    highest = lax.Precision.HIGHEST
    compensated = (gradients[0].astype(jnp.float32) + feedback[0].astype(jnp.float32)).astype(
        jnp.bfloat16
    )
    owner_count = lax.axis_size("mp")
    capacity = momentum.shape[1]
    matrices = owners.shape[0]
    replica_rows = momentum.shape[2]
    mp_index = lax.axis_index("mp")
    replica_index = lax.axis_index("replica")
    same_owner = owners[:, None] == owners[None, :]
    earlier = jnp.arange(matrices)[:, None] < jnp.arange(matrices)[None, :]
    ranks = jnp.sum((same_owner & earlier).astype(jnp.int32), axis=0)
    slots = owners * capacity + ranks
    slot_table = (slots[None, :] == jnp.arange(owner_count * capacity)[:, None]).astype(jnp.float32)
    table_narrow = slot_table.astype(jnp.bfloat16)
    table_mine = lax.dynamic_slice_in_dim(slot_table, mp_index * capacity, capacity, 0)
    left_terms = jnp.einsum(
        "kmn,knr->kmr", compensated, right_init, preferred_element_type=jnp.float32
    )
    left_sum = lax.psum(left_terms, "replica")
    left_rows = jnp.einsum("kmr,krs->kms", left_sum, gram_root, precision=highest).astype(
        jnp.bfloat16
    )
    right_terms = jnp.einsum(
        "kmn,kms->kns", compensated, left_rows, preferred_element_type=jnp.float32
    )
    right_new = lax.psum(right_terms, ("replica", "mp"))
    left_all = lax.all_gather(left_rows, "mp", axis=1, tiled=True)
    approx_rows = jnp.einsum(
        "kms,kns->kmn", left_rows.astype(jnp.float32), right_new, precision=highest
    )
    new_feedback = (compensated.astype(jnp.float32) - approx_rows).astype(jnp.bfloat16)
    left_chosen = jnp.einsum(
        "ck,kmr->cmr", table_mine.astype(jnp.bfloat16), left_all, preferred_element_type=jnp.float32
    )
    left_chosen = lax.dynamic_slice_in_dim(
        left_chosen, replica_index * replica_rows, replica_rows, 1
    )
    right_chosen = jnp.einsum("ck,knr->cnr", table_mine, right_new, precision=highest)
    approx_slots = jnp.einsum("cmr,cnr->cmn", left_chosen, right_chosen, precision=highest)
    new_momentum = 0.9 * momentum[0] + approx_slots
    new_master = master_weights[0] - 0.1 * new_momentum
    master_narrow = new_master.astype(jnp.bfloat16)
    weight_slots = lax.all_gather(master_narrow, "mp", axis=0, tiled=True)
    new_weights = jnp.einsum(
        "sk,smn->kmn", table_narrow, weight_slots, preferred_element_type=jnp.float32
    ).astype(jnp.bfloat16)
    vector_total = lax.psum(vector_grads[0], "replica")
    new_vector_momentum = 0.9 * vector_momentum + vector_total
    new_vector_params = vector_params - 0.1 * new_vector_momentum
    return (
        new_feedback[None],
        new_momentum[None],
        new_master[None],
        new_weights,
        new_vector_momentum,
        new_vector_params,
    )


def solution(mesh):
    return jax.shard_map(
        per_device,
        mesh=mesh,
        in_specs=(
            P("replica", None, "mp", None),
            P("replica", None, "mp", None),
            P(),
            P(),
            P(),
            P("mp", None, "replica", None),
            P("mp", None, "replica", None),
            P("replica", "mp"),
            P("mp"),
            P("mp"),
        ),
        out_specs=(
            P("replica", None, "mp", None),
            P("mp", None, "replica", None),
            P("mp", None, "replica", None),
            P(None, "replica", None),
            P("mp"),
            P("mp"),
        ),
        check_vma=False,
    )
```

profile of v0, /device:TPU:1, one launch (start us, length us, event | category | flops | bytes accessed | tf_op | source)
XLA Modules:
  0.0 481.2 jit_solution(16211220204946410669)
XLA Ops:
  7.2 0.0 copy-start
  7.2 0.0 all-reduce.3.cloned.1.call-start
  7.2 0.8 reduce.1
  8.0 0.6 copy-done
  8.6 0.0 copy-start.5
  8.6 3.1 fusion.27
  11.8 50.5 %all-reduce = (f32[8,48,32]{1,2,0:T(8,128)S(1)}, f32[672]{0:T(1024)S(1)}) all-reduce(f32[8,48,32]{1,2,0:T(8,128)S(1)} %fusion.27, f32[672]{0:T(1024)S(1)} %reduce.1), channel_id=1, replica_groups=mesh['replica'=16,'mp'=16] {'replica'}, use_global_device_ids=true, to_apply=%region_0.0 | all-reduce | flops 12960 | bytes 103680 | tf_op jit(solution)/shard_map/psum | solution.py:39
  62.2 0.0 copy-done.5
  62.3 0.4 convolution_convert_fusion
  62.6 4.7 fusion.25
  67.3 0.0 copy-start.8
  67.3 0.0 all-reduce.3.cloned.1.call-update
  67.4 0.0 all-gather.3.cloned.1.call-start
  67.4 0.1 copy.26
  67.6 0.4 copy-done.8
  68.0 0.1 convert_reduce_fusion
  68.1 22.7 %all_gather.6 = bf16[8,768,32]{2,0,1:T(8,128)(2,1)S(1)} all-gather(bf16[8,48,32]{2,0,1:T(8,128)(2,1)S(1)} %copy.26), channel_id=1, replica_groups=mesh['replica'=16,'mp'=16] {'mp'}, dimensions={1}, use_global_device_ids=true | all-gather | bytes 417792 | tf_op jit(solution)/shard_map/all_gather | solution.py:47
  90.8 1.1 multiply_reduce_fusion
  91.9 239.2 %all-reduce.3.cloned.1.call-done = f32[8,3072,32]{1,2,0:T(8,128)} async-done(((f32[8,3072,32]{1,2,0:T(8,128)}), f32[8,3072,32]{1,2,0:T(8,128)}) %all-reduce.3.cloned.1.call-update) | async-done | bytes 3145744 | tf_op jit(solution)/shard_map/psum | solution.py:46
  331.1 44.7 %fusion.6 = f32[1,3072,32]{0,1,2:T(8,128)} fusion(f32[8,3072,32]{1,2,0:T(8,128)} %all-reduce.3.cloned.1.call-done, pred[16,8]{1,0:T(8,128)(4,1)S(1)} %get-tuple-element.31, s32[]{:T(128)S(6)} %select_n.6), kind=kOutput, calls=%fused_computation.7 | convolution fusion | flops 9437184 | bytes 3539460 | tf_op jit(solution)/shard_map/ck,knr->cnr/dot_general | solution.py:58
  375.7 0.0 copy-start.3
  375.7 0.0 copy-start.4
  375.7 27.1 %copy.35 = f32[1,3072,32]{1,2,0:T(8,128)S(1)} copy(f32[1,3072,32]{0,1,2:T(8,128)} %fusion.6) | data formatting | bytes 786432 | tf_op jit(solution)/shard_map/ck,knr->cnr/dot_general | solution.py:58
  402.9 0.0 copy-done.3
  402.9 0.0 copy-start.6
  402.9 0.0 copy-start.7
  402.9 0.6 convolution_add_fusion
  403.6 0.0 copy-done.4
  403.6 0.0 copy-start.2
  403.6 1.2 fusion.10
  404.7 0.0 all-gather.3.cloned.1.call-update
  404.8 0.0 copy-done.6
  404.8 0.0 copy-done.7
  404.8 0.6 multiply_subtract_fusion
  405.4 7.4 %fusion.5 = bf16[1,8,48,3072]{3,2,1,0:T(8,128)(2,1)} fusion(bf16[8,48,32]{1,2,0:T(8,128)(2,1)S(1)} %convolution_convert_fusion, f32[8,3072,32]{1,2,0:T(8,128)} %all-reduce.3.cloned.1.call-done, bf16[1,8,48,3072]{3,2,1,0:T(8,128)(2,1)} %param.11, bf16[1,8,48,3072]{3,2,1,0:T(8,128)(2,1)} %param.10), kind=kOutput, calls=%fused_computation.5 | convolution fusion | flops 461242368 | bytes 10248192 | tf_op jit(solution)/shard_map/kms,kns->kmn/dot_general | solution.py:48
  412.8 0.0 copy-done.2
  412.8 51.4 %all-gather.3.cloned.1.call-done = bf16[768,3072]{1,0:T(8,128)(2,1)} async-done(((bf16[48,3072]{1,0:T(8,128)(2,1)}), bf16[768,3072]{1,0:T(8,128)(2,1)}) %all-gather.3.cloned.1.call-update) | async-done | bytes 4718608 | tf_op jit(solution)/shard_map/all_gather | solution.py:63
  464.2 0.0 copy-start.1
  464.2 7.5 %fusion.2 = bf16[8,48,3072]{2,0,1:T(8,128)(2,1)S(1)} fusion(bf16[16,48,3072]{2,1,0:T(8,128)(2,1)} %bitcast.41, s32[8]{0:T(128)S(1)} %add.27), kind=kOutput, calls=%fused_computation.4 | convolution fusion | flops 38928768 | bytes 7077920 | tf_op jit(solution)/shard_map/sk,smn->kmn/dot_general | solution.py:64
  471.7 2.7 copy.29
  474.4 0.0 copy-done.1
  (3 shorter events, 0.0 us)
Async XLA Ops:
  7.2 1.4 copy-start
  7.2 323.9 %all-reduce.3.cloned.1.call-start = ((), (), s32[]{:S(2)}) async-start(), calls=%async_computation | async-start | bytes 6291456 | tf_op jit(solution)/shard_map/psum | solution.py:46
  8.6 53.6 %copy-start.5 = (f32[8,32,32]{2,1,0:T(8,128)S(1)}, f32[8,32,32]{2,1,0:T(8,128)}, u32[]{:S(2)}) copy-start(f32[8,32,32]{2,1,0:T(8,128)} %param.13) | copy-start | bytes 98308
  67.3 0.7 copy-start.8
  67.4 396.9 %all-gather.3.cloned.1.call-start = ((), (), s32[]{:S(2)}) async-start(), calls=%async_computation.1 | async-start | bytes 5013504 | tf_op jit(solution)/shard_map/all_gather | solution.py:63
  375.7 27.1 %copy-start.3 = (f32[1,1,48,3072]{3,2,1,0:T(8,128)S(1)}, f32[1,1,48,3072]{3,2,1,0:T(8,128)}, u32[]{:S(2)}) copy-start(f32[1,1,48,3072]{3,2,1,0:T(8,128)} %param.15) | copy-start | bytes 1769476
  375.7 27.8 %copy-start.4 = (f32[1,1,48,3072]{3,2,1,0:T(8,128)S(1)}, f32[1,1,48,3072]{3,2,1,0:T(8,128)}, u32[]{:S(2)}) copy-start(f32[1,1,48,3072]{3,2,1,0:T(8,128)} %param.16) | copy-start | bytes 1769476
  402.9 1.9 copy-start.6
  402.9 1.9 copy-start.7
  403.6 9.2 %copy-start.2 = (f32[48,3072]{1,0:T(8,128)}, f32[48,3072]{1,0:T(8,128)S(1)}, u32[]{:S(2)}) copy-start(f32[48,3072]{1,0:T(8,128)S(1)} %convolution_add_fusion) | copy-start | bytes 1769476
  464.2 10.2 %copy-start.1 = (bf16[8,3072,32]{1,2,0:T(8,128)(2,1)S(1)}, bf16[8,3072,32]{1,2,0:T(8,128)(2,1)}, u32[]{:S(2)}) copy-start(bf16[8,3072,32]{1,2,0:T(8,128)(2,1)} %param.12) | copy-start | bytes 4718596
Sparse Core Ops, SparseCore 0:
  67.5 263.5 all-reduce.2
  404.9 59.2 all-gather.2
where the time goes:
time: 482 us; the launch traced here: 481 us
  waiting for transfers between devices  291 us (60%)
  blocking collectives  73.2 us (15%)
  matrix products  68.4 us (14%)
  local copies, waits for them, and re-layouts  31 us (6%)
  between operations  14.2 us (3%)
    psum x1, waiting for transfers between devices, per_device(): right_new = lax.psum(right_terms, ('replica', 'mp'))  239 us
    all_gather x1, waiting for transfers between devices, per_device(): weight_slots = lax.all_gather(master_narrow, 'mp', axis=0, tiled=True)  51.4 us
    psum x1, blocking collectives, per_device(): left_sum = lax.psum(left_terms, 'replica')  50.5 us
    dot_general x1, matrix products, per_device(): jnp.einsum('ck,knr->cnr', table_mine, right_new, precision=highest)  44.7 us
    dot_general x1, local copies, waits for them, and re-layouts, per_device(): jnp.einsum('ck,knr->cnr', table_mine, right_new, precision=highest)  27.1 us
    all_gather x1, blocking collectives, per_device(): left_all = lax.all_gather(left_rows, 'mp', axis=1, tiled=True)  22.7 us
  transfers between devices with their start and end apart: 2, of which 2 were waited for; matrix products, arithmetic and copies ran while one was open for 2% of the time, Pallas kernels for 0%

commit v1 on v0

--- a/solution.py
+++ b/solution.py
@@ -43,7 +43,7 @@
     right_terms = jnp.einsum(
         "kmn,kms->kns", compensated, left_rows, preferred_element_type=jnp.float32
     )
-    right_new = lax.psum(right_terms, ("replica", "mp"))
+    right_new = lax.psum(lax.psum(right_terms, "mp"), "replica")
     left_all = lax.all_gather(left_rows, "mp", axis=1, tiled=True)
     approx_rows = jnp.einsum(
         "kms,kns->kmn", left_rows.astype(jnp.float32), right_new, precision=highest

time: 482 us -> 444 us (0.921)
  waiting for transfers between devices: 291 us -> 256 us
    psum x1 -> x2, waiting for transfers between devices: 239 us -> 204 us  [per_device(): right_new = lax.psum(lax.psum(right_terms, 'mp'), 'replica')]
  transfers between devices with their start and end apart: 2 -> 3, of which waited for: 2 -> 3; matrix products, arithmetic and copies ran while one was open for 2% -> 2% of each run, Pallas kernels for 0% -> 0%
where the time goes in v1:
time: 444 us; the launch traced here: 443 us
  waiting for transfers between devices  256 us (58%)
  blocking collectives  70.6 us (16%)
  matrix products  68.4 us (15%)
  local copies, waits for them, and re-layouts  30.6 us (7%)
  between operations  13.9 us (3%)
    psum x2, waiting for transfers between devices, per_device(): right_new = lax.psum(lax.psum(right_terms, 'mp'), 'replica')  204 us
    all_gather x1, waiting for transfers between devices, per_device(): weight_slots = lax.all_gather(master_narrow, 'mp', axis=0, tiled=True)  51.7 us
    psum x1, blocking collectives, per_device(): left_sum = lax.psum(left_terms, 'replica')  50.5 us
    dot_general x1, matrix products, per_device(): jnp.einsum('ck,knr->cnr', table_mine, right_new, precision=highest)  44.7 us
    dot_general x1, local copies, waits for them, and re-layouts, per_device(): jnp.einsum('ck,knr->cnr', table_mine, right_new, precision=highest)  27.1 us
    all_gather x1, blocking collectives, per_device(): left_all = lax.all_gather(left_rows, 'mp', axis=1, tiled=True)  20.1 us
  transfers between devices with their start and end apart: 3, of which 3 were waited for; matrix products, arithmetic and copies ran while one was open for 2% of the time, Pallas kernels for 0%

profile of v1, /device:TPU:1, one launch (start us, length us, event | category | flops | bytes accessed | tf_op | source)
XLA Modules:
  0.0 443.4 jit_solution(10300548214776403722)
XLA Ops:
  7.2 0.0 copy-start
  7.2 0.0 all-reduce.4.cloned.1.call-start
  7.2 0.8 reduce.1
  8.0 0.6 copy-done
  8.6 0.0 copy-start.5
  8.6 3.1 fusion.27
  11.8 50.5 %all-reduce = (f32[8,48,32]{1,2,0:T(8,128)S(1)}, f32[672]{0:T(1024)S(1)}) all-reduce(f32[8,48,32]{1,2,0:T(8,128)S(1)} %fusion.27, f32[672]{0:T(1024)S(1)} %reduce.1), channel_id=1, replica_groups=mesh['replica'=16,'mp'=16] {'replica'}, use_global_device_ids=true, to_apply=%region_0.0 | all-reduce | flops 12960 | bytes 103680 | tf_op jit(solution)/shard_map/psum | solution.py:39
  62.2 0.0 copy-done.5
  62.3 0.4 convolution_convert_fusion
  62.6 4.7 %fusion.25 = f32[8,3072,32]{1,2,0:T(8,128)} fusion(bf16[8,48,32]{1,2,0:T(8,128)(2,1)S(1)} %convolution_convert_fusion, bf16[1,8,48,3072]{3,2,1,0:T(8,128)(2,1)} %param.11, bf16[1,8,48,3072]{3,2,1,0:T(8,128)(2,1)} %param.10), kind=kOutput, calls=%fused_computation.35 | convolution fusion | flops 80216064 | bytes 7888896 | tf_op jit(solution)/shard_map/kmn,kms->kns/dot_general | solution.py:43
  67.4 0.0 copy-start.8
  67.4 0.0 all-reduce.4.cloned.1.call-update
  67.4 0.0 all-reduce.6.cloned.1.call-start
  67.5 106.1 %all-reduce.4.cloned.1.call-done = f32[8,3072,32]{1,2,0:T(8,128)} async-done(((f32[8,3072,32]{1,2,0:T(8,128)}), f32[8,3072,32]{1,2,0:T(8,128)}) %all-reduce.4.cloned.1.call-update) | async-done | bytes 3145744 | tf_op jit(solution)/shard_map/psum | solution.py:46
  173.5 0.0 all-reduce.6.cloned.1.call-update
  173.5 0.0 all-gather.3.cloned.1.call-start
  173.6 0.1 copy.26
  173.7 0.0 copy-done.8
  173.7 0.1 convert_reduce_fusion
  173.8 20.1 %all_gather.6 = bf16[8,768,32]{2,0,1:T(8,128)(2,1)S(1)} all-gather(bf16[8,48,32]{2,0,1:T(8,128)(2,1)S(1)} %copy.26), channel_id=1, replica_groups=mesh['replica'=16,'mp'=16] {'mp'}, dimensions={1}, use_global_device_ids=true | all-gather | bytes 417792 | tf_op jit(solution)/shard_map/all_gather | solution.py:47
  194.0 1.1 multiply_reduce_fusion
  195.1 98.2 %all-reduce.6.cloned.1.call-done = f32[8,3072,32]{1,2,0:T(8,128)} async-done(((f32[8,3072,32]{1,2,0:T(8,128)}), f32[8,3072,32]{1,2,0:T(8,128)}) %all-reduce.6.cloned.1.call-update) | async-done | bytes 3145744 | tf_op jit(solution)/shard_map/psum | solution.py:46
  293.4 44.7 %fusion.6 = f32[1,3072,32]{0,1,2:T(8,128)} fusion(f32[8,3072,32]{1,2,0:T(8,128)} %all-reduce.6.cloned.1.call-done, pred[16,8]{1,0:T(8,128)(4,1)S(1)} %get-tuple-element.31, s32[]{:T(128)S(6)} %select_n.6), kind=kOutput, calls=%fused_computation.7 | convolution fusion | flops 9437184 | bytes 3539460 | tf_op jit(solution)/shard_map/ck,knr->cnr/dot_general | solution.py:58
  338.0 0.0 copy-start.3
  338.0 0.0 copy-start.4
  338.0 27.1 %copy.35 = f32[1,3072,32]{1,2,0:T(8,128)S(1)} copy(f32[1,3072,32]{0,1,2:T(8,128)} %fusion.6) | data formatting | bytes 786432 | tf_op jit(solution)/shard_map/ck,knr->cnr/dot_general | solution.py:58
  365.2 0.0 copy-done.3
  365.2 0.0 copy-start.6
  365.2 0.0 copy-start.7
  365.2 0.6 convolution_add_fusion
  365.8 0.0 copy-done.4
  365.8 0.0 copy-start.2
  365.8 1.2 fusion.10
  367.0 0.0 all-gather.3.cloned.1.call-update
  367.0 0.0 copy-done.6
  367.0 0.0 copy-done.7
  367.1 0.6 multiply_subtract_fusion
  367.7 7.4 %fusion.5 = bf16[1,8,48,3072]{3,2,1,0:T(8,128)(2,1)} fusion(bf16[8,48,32]{1,2,0:T(8,128)(2,1)S(1)} %convolution_convert_fusion, f32[8,3072,32]{1,2,0:T(8,128)} %all-reduce.6.cloned.1.call-done, bf16[1,8,48,3072]{3,2,1,0:T(8,128)(2,1)} %param.11, bf16[1,8,48,3072]{3,2,1,0:T(8,128)(2,1)} %param.10), kind=kOutput, calls=%fused_computation.5 | convolution fusion | flops 461242368 | bytes 10248192 | tf_op jit(solution)/shard_map/kms,kns->kmn/dot_general | solution.py:48
  375.1 0.0 copy-done.2
  375.1 51.7 %all-gather.3.cloned.1.call-done = bf16[768,3072]{1,0:T(8,128)(2,1)} async-done(((bf16[48,3072]{1,0:T(8,128)(2,1)}), bf16[768,3072]{1,0:T(8,128)(2,1)}) %all-gather.3.cloned.1.call-update) | async-done | bytes 4718608 | tf_op jit(solution)/shard_map/all_gather | solution.py:63
  426.7 0.0 copy-start.1
  426.7 7.5 %fusion.2 = bf16[8,48,3072]{2,0,1:T(8,128)(2,1)S(1)} fusion(bf16[16,48,3072]{2,1,0:T(8,128)(2,1)} %bitcast.41, s32[8]{0:T(128)S(1)} %add.29), kind=kOutput, calls=%fused_computation.4 | convolution fusion | flops 38928768 | bytes 7077920 | tf_op jit(solution)/shard_map/sk,smn->kmn/dot_general | solution.py:64
  434.2 2.7 copy.29
  436.9 0.0 copy-done.1
  (3 shorter events, 0.0 us)
Async XLA Ops:
  7.2 1.4 copy-start
  7.2 166.3 %all-reduce.4.cloned.1.call-start = ((), (), s32[]{:S(2)}) async-start(), calls=%async_computation | async-start | bytes 6291456 | tf_op jit(solution)/shard_map/psum | solution.py:46
  8.6 53.6 %copy-start.5 = (f32[8,32,32]{2,1,0:T(8,128)S(1)}, f32[8,32,32]{2,1,0:T(8,128)}, u32[]{:S(2)}) copy-start(f32[8,32,32]{2,1,0:T(8,128)} %param.13) | copy-start | bytes 98308
  67.4 106.3 %copy-start.8 = (s32[8]{0:T(128)S(1)}, s32[8]{0:T(128)}, u32[]{:S(2)}) copy-start(s32[8]{0:T(128)} %param.14) | copy-start | bytes 100
  67.4 225.9 %all-reduce.6.cloned.1.call-start = ((), (), s32[]{:S(2)}) async-start(), calls=%async_computation.1 | async-start | bytes 6291456 | tf_op jit(solution)/shard_map/psum | solution.py:46
  173.5 253.2 %all-gather.3.cloned.1.call-start = ((), (), s32[]{:S(2)}) async-start(), calls=%async_computation.2 | async-start | bytes 5013504 | tf_op jit(solution)/shard_map/all_gather | solution.py:63
  338.0 27.1 %copy-start.3 = (f32[1,1,48,3072]{3,2,1,0:T(8,128)S(1)}, f32[1,1,48,3072]{3,2,1,0:T(8,128)}, u32[]{:S(2)}) copy-start(f32[1,1,48,3072]{3,2,1,0:T(8,128)} %param.15) | copy-start | bytes 1769476
  338.0 27.8 %copy-start.4 = (f32[1,1,48,3072]{3,2,1,0:T(8,128)S(1)}, f32[1,1,48,3072]{3,2,1,0:T(8,128)}, u32[]{:S(2)}) copy-start(f32[1,1,48,3072]{3,2,1,0:T(8,128)} %param.16) | copy-start | bytes 1769476
  365.2 1.9 copy-start.6
  365.2 1.9 copy-start.7
  365.8 9.2 %copy-start.2 = (f32[48,3072]{1,0:T(8,128)}, f32[48,3072]{1,0:T(8,128)S(1)}, u32[]{:S(2)}) copy-start(f32[48,3072]{1,0:T(8,128)S(1)} %convolution_add_fusion) | copy-start | bytes 1769476
  426.7 10.2 %copy-start.1 = (bf16[8,3072,32]{1,2,0:T(8,128)(2,1)S(1)}, bf16[8,3072,32]{1,2,0:T(8,128)(2,1)}, u32[]{:S(2)}) copy-start(bf16[8,3072,32]{1,2,0:T(8,128)(2,1)} %param.12) | copy-start | bytes 4718596
Sparse Core Ops, SparseCore 0:
  67.5 105.9 all-reduce.3
  175.9 117.4 all-reduce.5
  367.2 59.5 all-gather.2
